TPU v7x, 256 devices: a whole 4x4x8 slice. The times are simulated.
256 devices in a mesh: ctx: 8 (over z), chan: 32 (over x, y, core).
Axes of the slice: x: 4, y: 4, z: 8, core: 2. Of those that a mesh axis runs over, the one named last changes fastest.
Arguments:
- query_rows: bfloat16 [2048, 8192], P('ctx', 'chan'), may hold values from -6 to 6
- key_rows: bfloat16 [2048, 8192], P('ctx', 'chan'), may hold values from -6 to 6
- value_rows: bfloat16 [2048, 8192], P('ctx', 'chan'), may hold values from -6 to 6
- short_taps: float32 [3, 3, 8192], P(None, None, 'chan'), may hold values from -3 to 3
- long_filter: bfloat16 [2048, 8192], P('ctx', 'chan'), may hold values from -4 to 4
- direction: bfloat16 [2048, 8192], P('ctx', 'chan'), may hold values from -4 to 4
- w_out: bfloat16 [8192, 8192], P('chan'), may hold values from -0.125 to 0.125
- target: bfloat16 [2048, 8192], P('ctx'), may hold values from -6 to 6
Outputs:
- grad_filter: float32 [2048, 8192], P('ctx', 'chan')
- hvp_filter: float32 [2048, 8192], P('ctx', 'chan')
All inputs are finite; a program needn't handle non-finite values.
Results may differ from a plain program's by a relative error of at most 0.033.
Values may be sent and summed in bfloat16 or wider, within the bound.
A program may use at most 128 MiB of HBM per device.

v0:
```python
import math
import jax
import jax.numpy as jnp
from jax import lax
from jax.sharding import PartitionSpec as P


def passed_along(value, axis, steps):
    count = lax.axis_size(axis)
    initial, last = (max(0, -steps), min(count, count - steps))
    return lax.ppermute(value, axis, [(source, source + steps) for source in range(initial, last)])


def short_conv(current, earlier, coeffs):
    extended = jnp.concatenate([earlier.astype(jnp.float32), current.astype(jnp.float32)], axis=0)
    length = current.shape[0]
    return (
        coeffs[0] * extended[2 : 2 + length]
        + coeffs[1] * extended[1 : 1 + length]
        + coeffs[2] * extended[0:length]
    )


def depthwise(window, kernel):
    result = lax.conv_general_dilated(
        window[None],
        kernel[:, None, :],
        (1,),
        "VALID",
        dimension_numbers=("NHC", "HIO", "NHC"),
        feature_group_count=window.shape[1],
        preferred_element_type=jnp.float32,
    )
    return result[0]


def paired(window, first_kernel, second_kernel):
    return jax.vmap(lambda kernel: depthwise(window, kernel))(
        jnp.stack([first_kernel, second_kernel])
    )


def on_device(query_rows, key_rows, value_rows, short_taps, long_filter, direction, w_out, target):
    block_len = query_rows.shape[0]
    chan_width = query_rows.shape[1]
    earlier = passed_along(
        (query_rows[block_len - 2 :], key_rows[block_len - 2 :], value_rows[block_len - 2 :]),
        "ctx",
        1,
    )
    taps_all, dir_all = (
        lax.all_gather(long_filter, "ctx", axis=0, tiled=True),
        lax.all_gather(direction, "ctx", axis=0, tiled=True),
    )
    gate_in = short_conv(query_rows, earlier[0], short_taps[0])
    key_short = short_conv(key_rows, earlier[1], short_taps[1])
    value_short = short_conv(value_rows, earlier[2], short_taps[2])
    mixed_rows = (key_short * value_short).astype(jnp.bfloat16)
    history = lax.all_gather(mixed_rows, "ctx", axis=0, tiled=True)
    seq_total = history.shape[0]
    my_block = lax.axis_index("ctx")
    padded = jnp.concatenate([jnp.zeros((block_len, chan_width), jnp.bfloat16), history], axis=0)

    def window_at(distance):
        return lax.dynamic_slice_in_dim(padded, distance * block_len + 1, 2 * block_len - 1, 0)

    def forward_step(tap_block, running):
        window = window_at(my_block - tap_block)
        taps_here = lax.dynamic_slice_in_dim(taps_all, tap_block * block_len, block_len, 0)[::-1]
        dirs_here = lax.dynamic_slice_in_dim(dir_all, tap_block * block_len, block_len, 0)[::-1]
        return running + paired(window, taps_here, dirs_here)

    convolved = lax.fori_loop(
        0, my_block + 1, forward_step, jnp.zeros((2, block_len, chan_width), jnp.float32)
    )
    gated_rows = (gate_in * convolved[0]).astype(jnp.bfloat16)
    gated_dir = (gate_in * convolved[1]).astype(jnp.bfloat16)
    stacked = jnp.concatenate([gated_rows, gated_dir], axis=0)
    scaling = 1.0 / math.sqrt(seq_total)
    summed = lax.psum_scatter(
        lax.dot_general(
            w_out, stacked, (((0,), (1,)), ((), ())), preferred_element_type=jnp.float32
        ).astype(jnp.bfloat16),
        "chan",
        scatter_dimension=0,
        tiled=True,
    ).astype(jnp.float32)
    column_start = lax.axis_index("chan") * chan_width
    target_mine = (
        lax.dynamic_slice_in_dim(target, column_start, chan_width, 1).astype(jnp.float32).T
    )
    bent_out = jnp.tanh(summed[:, :block_len] - target_mine)
    cot_grad = (scaling * bent_out).astype(jnp.bfloat16)
    cot_hvp = (scaling * (1.0 - bent_out * bent_out) * summed[:, block_len:]).astype(jnp.bfloat16)
    cotangent = jnp.concatenate([cot_grad, cot_hvp], axis=1)
    backward = jnp.dot(
        w_out,
        lax.all_gather(cotangent, "chan", axis=0, tiled=True),
        preferred_element_type=jnp.float32,
    )
    back_grad = backward[:, :block_len].T
    back_hvp = backward[:, block_len:].T
    dz_grad = (gate_in * back_grad).astype(jnp.bfloat16)
    dz_hvp = (gate_in * back_hvp).astype(jnp.bfloat16)

    def backward_step(tap_block, running):
        window = window_at(my_block - tap_block)
        pair = paired(window, dz_grad, dz_hvp)[:, ::-1]
        placed = jnp.concatenate([pair[0], pair[1]], axis=1)
        return lax.dynamic_update_slice_in_dim(running, placed, tap_block * block_len, 0)

    tap_terms = lax.fori_loop(
        0, my_block + 1, backward_step, jnp.zeros((seq_total, 2 * chan_width), jnp.float32)
    )
    shares = lax.psum_scatter(
        tap_terms.astype(jnp.bfloat16), "ctx", scatter_dimension=0, tiled=True
    ).astype(jnp.float32)
    return (shares[:, :chan_width], shares[:, chan_width:])


def solution(mesh):
    in_specs = (
        P("ctx", "chan"),
        P("ctx", "chan"),
        P("ctx", "chan"),
        P(None, None, "chan"),
        P("ctx", "chan"),
        P("ctx", "chan"),
        P("chan", None),
        P("ctx", None),
    )
    out_specs = (P("ctx", "chan"), P("ctx", "chan"))
    return jax.shard_map(
        on_device, mesh=mesh, in_specs=in_specs, out_specs=out_specs, check_vma=False
    )
```

profile of v0, /device:TPU:2, one launch (start us, length us, event | category | flops | bytes accessed | tf_op | source)
XLA Modules:
  0.0 615.9 jit_solution(8180843435490185184)
XLA Ops:
  7.2 0.7 slice.125
  7.9 3.8 collective-permute-start
  11.7 0.7 slice.131
  12.4 3.8 collective-permute-start.1
  16.2 1.5 fusion.41
  17.7 0.9 convert_element_type.55
  18.6 0.9 convert_element_type.57
  19.6 0.8 fusion.14
  20.5 0.7 all-gather.7.cloned.1.call-update
  22.0 0.7 slice.137
  22.7 3.8 collective-permute-start.2
  26.5 1.6 convert_element_type.60
  28.7 31.8 %all-gather.5.cloned.1.call-done = bf16[2048,256]{1,0:T(8,128)(2,1)} async-done(((bf16[256,256]{1,0:T(8,128)(2,1)}), bf16[2048,256]{1,0:T(8,128)(2,1)}) %all-gather.5.cloned.1.call-update) | async-done | bytes 1048592 | tf_op jit(solution)/shard_map/all_gather | solution.py:59
  60.6 1.3 concatenate.26
  61.9 37.3 %all-gather.7.cloned.1.call-done = bf16[2048,256]{1,0:T(8,128)(2,1)} async-done(((bf16[256,256]{1,0:T(8,128)(2,1)}), bf16[2048,256]{1,0:T(8,128)(2,1)}) %all-gather.7.cloned.1.call-update) | async-done | bytes 1048592 | tf_op jit(solution)/shard_map/all_gather | solution.py:52
  99.2 38.6 %all-gather.9.cloned.1.call-done = bf16[2048,256]{1,0:T(8,128)(2,1)} async-done(((bf16[256,256]{1,0:T(8,128)(2,1)}), bf16[2048,256]{1,0:T(8,128)(2,1)}) %all-gather.9.cloned.1.call-update) | async-done | bytes 1048592 | tf_op jit(solution)/shard_map/all_gather | solution.py:53
  138.0 15.6 %while.24 = (s32[]{:T(128)}, f32[2,256,256]{2,0,1:T(2,128)S(1)}, s32[]{:T(128)}, s32[]{:T(128)}, bf16[2304,256]{1,0:T(8,128)(2,1)S(1)}, /*index=5*/bf16[2048,256...) while((s32[]{:T(128)}, f32[2,256,256]{2,0,1:T(2,128)S(1)}, ...), condition=%wide.region_1.0_spmd, body=%wide.region_0.0_spmd.sunk | while | flops 67371016 | bytes 4717297 | solution.py:73
  138.0 1.0 constant_dynamic-slice_fusion.3
  139.6 13.5 %convolution_bitcast_fusion.5 = f32[2,1,256,256]{3,1,0,2:T(1,128)S(1)} fusion(bf16[256,1,256,2]{2,0,3,1:T(8,128)(2,1)S(1)} %maximum_bitcast_fusion.2, bf16[1,511,256,1]{2,1,3,0:T(8,128)(2,1)S(1)} %dynamic-slice_bitcast_fusion.4), kind=kOutput, calls=%fused_computation.clone.1 | convolution fusion | flops 67108864 | bytes 1048064 | tf_op jit(solution)/shard_map/convolution.6
  153.9 7.8 %fusion.4 = bf16[8192,512]{0,1:T(8,128)(2,1)} fusion(bf16[256,8192]{1,0:T(8,128)(2,1)} %param.18, bf16[256,256]{1,0:T(8,128)(2,1)S(1)} %fusion.26, bf16[256,256]{1,0:T(8,128)(2,1)S(1)} %get-tuple-element.225), kind=kOutput, calls=%fused_computation.17 | convolution fusion | flops 2152202240 | bytes 12845056 | tf_op jit(solution)/shard_map/dot_general | solution.py:81
  161.8 206.3 %reduce-scatter.3.cloned.1.call-done = bf16[256,512]{0,1:T(8,128)(2,1)} async-done(((bf16[8192,512]{0,1:T(8,128)(2,1)}), bf16[256,512]{0,1:T(8,128)(2,1)}) %reduce-scatter.3.cloned.1.call-update) | async-done | bytes 262160 | tf_op jit(solution)/shard_map/reduce_scatter | solution.py:80
  368.0 1.0 convert_element_type.66
  369.0 1.0 multiply_convert_fusion
  370.0 0.7 pad_maximum_fusion.3
  371.0 63.1 %all-gather.11.cloned.1.call-done = bf16[8192,512]{0,1:T(8,128)(2,1)} async-done(((bf16[256,512]{0,1:T(8,128)(2,1)}), bf16[8192,512]{0,1:T(8,128)(2,1)}) %all-gather.11.cloned.1.call-update) | async-done | bytes 8388624 | tf_op jit(solution)/shard_map/all_gather | solution.py:98
  434.1 6.9 %convolution_bitcast_fusion.2 = f32[256,512]{0,1:T(8,128)S(1)} fusion(bf16[8192,512]{0,1:T(8,128)(2,1)} %all-gather.11.cloned.1.call-done, bf16[256,8192]{1,0:T(8,128)(2,1)} %param.18), kind=kOutput, calls=%fused_computation.18 | convolution fusion | flops 2147483648 | bytes 13107200 | tf_op jit(solution)/shard_map/dot_general | solution.py:96
  441.4 1.5 broadcast_in_dim.21
  442.9 15.5 %while.25 = (s32[]{:T(128)}, bf16[2048,512]{1,0:T(8,128)(2,1)}, s32[]{:T(128)}, s32[]{:T(128)}, bf16[2304,256]{1,0:T(8,128)(2,1)S(1)}, /*index=5*/bf16[2,256,256...) while((s32[]{:T(128)}, bf16[2048,512]{1,0:T(8,128)(2,1)}, ...), condition=%wide.region_4.0_spmd, body=%wide.region_3.0_spmd.sunk | while | flops 67633160 | bytes 3406569 | solution.py:112
  442.9 13.6 %convolution_bitcast_fusion.6 = bf16[2,1,256,256]{3,1,0,2:T(2,128)(2,1)S(1)} fusion(bf16[256,1,256,2]{2,3,0,1:T(2,128)(2,1)S(1)} %bitcast.127, bf16[1,511,256,1]{2,1,3,0:T(8,128)(2,1)S(1)} %dynamic-slice_bitcast_fusion.5), kind=kOutput, calls=%fused_computation.8.clone.1 | convolution fusion | flops 67108864 | bytes 785920 | tf_op jit(solution)/shard_map/convolution.7
  457.6 0.7 maximum_dynamic-update-slice_fusion.2
  458.4 148.9 %reduce-scatter.5.cloned.1.call-done = bf16[256,512]{1,0:T(8,128)(2,1)} async-done(((bf16[2048,512]{1,0:T(8,128)(2,1)}), bf16[256,512]{1,0:T(8,128)(2,1)}) %reduce-scatter.5.cloned.1.call-update) | async-done | bytes 262160 | tf_op jit(solution)/shard_map/reduce_scatter | solution.py:115
  607.2 1.8 fusion.40
  (45 shorter events, 4.6 us)
Async XLA Ops:
  7.2 53.4 %all-gather.5.cloned.1.call-start = ((), (), s32[]{:S(2)}) async-start(), calls=%async_computation.2 | async-start | bytes 1179648 | tf_op jit(solution)/shard_map/all_gather | solution.py:59
  7.9 11.6 %collective-permute-start = (bf16[2,256]{1,0:T(2,128)(2,1)S(1)}, bf16[2,256]{1,0:T(2,128)(2,1)S(1)}, u32[]{:S(2)}, u32[]{:S(2)}) collective-permute-start(bf16[2,256]{1,0:T(2,128)(2,1)S(1)} %slice.125), channel_id=1, source_target_pairs={{0,32},{32,64},{64,96},{96,128},{128,160},{160,192},{192,224},{1,3... | collective-permute-start | bytes 3080 | tf_op jit(solution)/shard_map/ppermute | solution.py:11
  12.4 7.2 %collective-permute-start.1 = (bf16[2,256]{1,0:T(2,128)(2,1)S(1)}, bf16[2,256]{1,0:T(2,128)(2,1)S(1)}, u32[]{:S(2)}, u32[]{:S(2)}) collective-permute-start(bf16[2,256]{1,0:T(2,128)(2,1)S(1)} %slice.131), channel_id=1, source_target_pairs={{0,32},{32,64},{64,96},{96,128},{128,160},{160,192},{192,224},{1,3... | collective-permute-start | bytes 3080 | tf_op jit(solution)/shard_map/ppermute | solution.py:11
  20.4 78.7 %all-gather.7.cloned.1.call-start = ((), (), s32[]{:S(2)}) async-start(), calls=%async_computation.3 | async-start | bytes 1179648 | tf_op jit(solution)/shard_map/all_gather | solution.py:52
  21.2 116.6 %all-gather.9.cloned.1.call-start = ((), (), s32[]{:S(2)}) async-start(), calls=%async_computation.4 | async-start | bytes 1179648 | tf_op jit(solution)/shard_map/all_gather | solution.py:53
  21.9 346.1 %reduce-scatter.3.cloned.1.call-start = ((), (), s32[]{:S(2)}) async-start(), calls=%async_computation.5 | async-start | bytes 8650752 | tf_op jit(solution)/shard_map/reduce_scatter | solution.py:80
  22.7 5.5 collective-permute-start.2
  138.0 15.7 %copy-start = (f32[256,256]{1,0:T(8,128)S(1)}, f32[256,256]{1,0:T(8,128)}, u32[]{:S(2)}) copy-start(f32[256,256]{1,0:T(8,128)} %convert_element_type.60) | copy-start | bytes 786436
  138.0 15.7 %copy-start.1 = (f32[2,256]{1,0:T(2,128)S(1)}, f32[2,256]{1,0:T(2,128)}, u32[]{:S(2)}) copy-start(f32[2,256]{1,0:T(2,128)} %convert_element_type.61) | copy-start | bytes 6148
  138.0 15.7 %copy-start.2 = (f32[1,1,256]{2,1,0:T(1,128)S(1)}, f32[1,1,256]{2,1,0:T(1,128)}, u32[]{:S(2)}) copy-start(f32[1,1,256]{2,1,0:T(1,128)} %get-tuple-element.237) | copy-start | bytes 3076
  138.0 15.7 %copy-start.3 = (f32[1,1,256]{2,1,0:T(1,128)S(1)}, f32[1,1,256]{2,1,0:T(1,128)}, u32[]{:S(2)}) copy-start(f32[1,1,256]{2,1,0:T(1,128)} %get-tuple-element.244) | copy-start | bytes 3076
  138.0 15.7 %copy-start.4 = (f32[1,1,256]{2,1,0:T(1,128)S(1)}, f32[1,1,256]{2,1,0:T(1,128)}, u32[]{:S(2)}) copy-start(f32[1,1,256]{2,1,0:T(1,128)} %get-tuple-element.245) | copy-start | bytes 3076
  161.7 272.4 %all-gather.11.cloned.1.call-start = ((), (), s32[]{:S(2)}) async-start(), calls=%async_computation.6 | async-start | bytes 8650752 | tf_op jit(solution)/shard_map/all_gather | solution.py:98
  370.8 236.5 %reduce-scatter.5.cloned.1.call-start = ((), (), s32[]{:S(2)}) async-start(), calls=%async_computation.7 | async-start | bytes 2359296 | tf_op jit(solution)/shard_map/reduce_scatter | solution.py:115
Sparse Core Ops, SparseCore 0:
  20.6 39.9 all-gather.4
  62.4 36.7 all-gather.6
  101.0 36.7 all-gather.8
  161.8 206.1 reduce-scatter.2
  370.9 63.1 all-gather.10
  458.5 148.7 reduce-scatter.4
where the time goes:
time: 616 us
  waiting for transfers between devices  527 us (86%)
  matrix products  41.8 us (7%)
  between operations  14.3 us (2%)
  starting transfers between devices  11.9 us (2%)
  local copies, waits for them, and re-layouts  11.1 us (2%)
  other arithmetic  9.17 us (1%)
    reduce_scatter x1, waiting for transfers between devices, on_device(): lax.psum_scatter(lax.dot_general(w_out, stacked, (((0,), (1,)), ((), ()))...  206 us
    reduce_scatter x1, waiting for transfers between devices, on_device(): lax.psum_scatter(tap_terms.astype(jnp.bfloat16), 'ctx', scatter_dimension...  149 us
    all_gather x1, waiting for transfers between devices, on_device(): lax.all_gather(cotangent, 'chan', axis=0, tiled=True)  63.1 us
    all_gather x1, waiting for transfers between devices, on_device(): lax.all_gather(direction, 'ctx', axis=0, tiled=True)  38.6 us
    all_gather x1, waiting for transfers between devices, on_device(): lax.all_gather(long_filter, 'ctx', axis=0, tiled=True)  37.3 us
    all_gather x1, waiting for transfers between devices, on_device(): history = lax.all_gather(mixed_rows, 'ctx', axis=0, tiled=True)  31.8 us
    another operation x2, matrix products  27.1 us
  transfers between devices with their start and end apart: 9, of which 6 were waited for; matrix products, arithmetic and copies ran while one was open for 1% of the time, Pallas kernels for 0%

commit v1 on v0

--- a/solution.py
+++ b/solution.py
@@ -56,7 +56,16 @@
     key_short = short_conv(key_rows, earlier[1], short_taps[1])
     value_short = short_conv(value_rows, earlier[2], short_taps[2])
     mixed_rows = (key_short * value_short).astype(jnp.bfloat16)
-    history = lax.all_gather(mixed_rows, "ctx", axis=0, tiled=True)
+
+    def build_trails(local_block):
+        return jnp.concatenate(
+            lax.all_to_all(
+                jnp.stack([local_block for _ in range(lax.psum(1, "ctx"))]), "ctx", 0, 0
+            ),
+            axis=0,
+        )
+
+    history = build_trails(mixed_rows)
     seq_total = history.shape[0]
     my_block = lax.axis_index("ctx")
     padded = jnp.concatenate([jnp.zeros((block_len, chan_width), jnp.bfloat16), history], axis=0)

time: 616 us -> 580 us (0.942)
  waiting for transfers between devices: 527 us -> 486 us
  starting transfers between devices: 11.9 us -> 19 us
    all_gather x1, waiting for transfers between devices: 37.3 us -> 0.02 us  [on_device(): lax.all_gather(long_filter, 'ctx', axis=0, tiled=True)]
    all_gather x1 -> x0, waiting for transfers between devices: 31.8 us -> none  [on_device(): history = lax.all_gather(mixed_rows, 'ctx', axis=0, tiled=True)]
    ppermute x3, waiting for transfers between devices: 0.01 us -> 22.2 us  [passed_along(): lax.ppermute(value, axis, [(source, source + steps) for source in range(i...]
    all_to_all x0 -> x1, starting transfers between devices: none -> 7.07 us  [build_trails(): lax.all_to_all(jnp.stack([local_block for _ in range(lax.psum(1, 'ctx'))]...]
where the time goes in v1:
time: 580 us; the launch traced here: 579 us
  waiting for transfers between devices  486 us (84%)
  matrix products  41.8 us (7%)
  starting transfers between devices  19 us (3%)
  between operations  14 us (2%)
  local copies, waits for them, and re-layouts  10.3 us (2%)
  other arithmetic  7.59 us (1%)
    reduce_scatter x1, waiting for transfers between devices, on_device(): lax.psum_scatter(lax.dot_general(w_out, stacked, (((0,), (1,)), ((), ()))...  206 us
    reduce_scatter x1, waiting for transfers between devices, on_device(): lax.psum_scatter(tap_terms.astype(jnp.bfloat16), 'ctx', scatter_dimension...  149 us
    all_gather x1, waiting for transfers between devices, on_device(): lax.all_gather(cotangent, 'chan', axis=0, tiled=True)  63.1 us
    all_gather x1, waiting for transfers between devices, on_device(): lax.all_gather(direction, 'ctx', axis=0, tiled=True)  39.4 us
    another operation x2, matrix products  27.1 us
    ppermute x3, waiting for transfers between devices, passed_along(): lax.ppermute(value, axis, [(source, source + steps) for source in range(i...  22.2 us
  transfers between devices with their start and end apart: 9, of which 6 were waited for; matrix products, arithmetic and copies ran while one was open for 1% of the time, Pallas kernels for 0%

profile of v1, /device:TPU:2, one launch (start us, length us, event | category | flops | bytes accessed | tf_op | source)
XLA Modules:
  0.0 579.1 jit_solution(885201320377437420)
XLA Ops:
  7.2 0.7 all-gather.4.cloned.1.call-update
  7.9 0.7 slice.125
  8.6 3.8 collective-permute-start
  12.4 0.7 slice.131
  13.1 3.8 collective-permute-start.1
  16.9 1.4 fusion.41
  18.4 0.9 convert_element_type.55
  19.3 0.9 convert_element_type.57
  20.5 1.1 stack.44
  21.5 7.1 %all-to-all-start = ((bf16[8,256,256]{2,1,0:T(8,128)(2,1)}), bf16[8,256,256]{2,1,0:T(8,128)(2,1)S(1)}, u32[]{:S(2)}, u32[]{:S(2)}) async-start(bf16[8,256,256]{2,1,0:T(8,128)(2,1)} %stack.44), calls=%async_computation | async-start | bytes 2097152 | tf_op jit(solution)/shard_map/all_to_all | solution.py:62
  28.6 0.7 all-gather.6.cloned.1.call-update
  29.4 3.9 collective-permute-start.2
  33.3 0.7 convert_element_type.60
  34.0 22.2 %collective-permute-done.2 = bf16[2,256]{1,0:T(2,128)(2,1)S(1)} collective-permute-done((bf16[2,256]{1,0:T(2,128)(2,1)S(1)}, bf16[2,256]{1,0:T(2,128)(2,1)S(1)}, u32[]{:S(2)}, u32[]{:S(2)}) %collective-permute-start.2) | collective-permute-done | bytes 1056 | tf_op jit(solution)/shard_map/ppermute | solution.py:11
  56.8 5.0 all-to-all-done
  61.9 39.4 %all-gather.6.cloned.1.call-done = bf16[2048,256]{1,0:T(8,128)(2,1)} async-done(((bf16[256,256]{1,0:T(8,128)(2,1)}), bf16[2048,256]{1,0:T(8,128)(2,1)}) %all-gather.6.cloned.1.call-update) | async-done | bytes 1048592 | tf_op jit(solution)/shard_map/all_gather | solution.py:53
  101.5 15.6 %while.24 = (s32[]{:T(128)}, f32[2,256,256]{2,0,1:T(2,128)S(1)}, s32[]{:T(128)}, s32[]{:T(128)}, bf16[2304,256]{1,0:T(8,128)(2,1)S(1)}, /*index=5*/bf16[2048,256...) while((s32[]{:T(128)}, f32[2,256,256]{2,0,1:T(2,128)S(1)}, ...), condition=%wide.region_1.0_spmd, body=%wide.region_0.0_spmd.sunk | while | flops 67371016 | bytes 4717297 | solution.py:82
  101.5 1.0 constant_dynamic-slice_fusion.3
  103.1 13.5 %convolution_bitcast_fusion.5 = f32[2,1,256,256]{3,1,0,2:T(1,128)S(1)} fusion(bf16[256,1,256,2]{2,0,3,1:T(8,128)(2,1)S(1)} %maximum_bitcast_fusion.2, bf16[1,511,256,1]{2,1,3,0:T(8,128)(2,1)S(1)} %dynamic-slice_bitcast_fusion.4), kind=kOutput, calls=%fused_computation.clone.1 | convolution fusion | flops 67108864 | bytes 1048064 | tf_op jit(solution)/shard_map/convolution.6
  117.4 7.8 %fusion.4 = bf16[8192,512]{0,1:T(8,128)(2,1)} fusion(bf16[256,8192]{1,0:T(8,128)(2,1)} %param.18, bf16[256,256]{1,0:T(8,128)(2,1)S(1)} %fusion.26, bf16[256,256]{1,0:T(8,128)(2,1)S(1)} %get-tuple-element.225), kind=kOutput, calls=%fused_computation.17 | convolution fusion | flops 2152202240 | bytes 12845056 | tf_op jit(solution)/shard_map/dot_general | solution.py:90
  125.3 206.3 %reduce-scatter.3.cloned.1.call-done = bf16[256,512]{0,1:T(8,128)(2,1)} async-done(((bf16[8192,512]{0,1:T(8,128)(2,1)}), bf16[256,512]{0,1:T(8,128)(2,1)}) %reduce-scatter.3.cloned.1.call-update) | async-done | bytes 262160 | tf_op jit(solution)/shard_map/reduce_scatter | solution.py:89
  331.5 1.0 convert_element_type.66
  332.5 1.0 multiply_convert_fusion
  333.5 0.7 pad_maximum_fusion.3
  334.5 63.1 %all-gather.8.cloned.1.call-done = bf16[8192,512]{0,1:T(8,128)(2,1)} async-done(((bf16[256,512]{0,1:T(8,128)(2,1)}), bf16[8192,512]{0,1:T(8,128)(2,1)}) %all-gather.8.cloned.1.call-update) | async-done | bytes 8388624 | tf_op jit(solution)/shard_map/all_gather | solution.py:107
  397.6 6.9 %convolution_bitcast_fusion.2 = f32[256,512]{0,1:T(8,128)S(1)} fusion(bf16[8192,512]{0,1:T(8,128)(2,1)} %all-gather.8.cloned.1.call-done, bf16[256,8192]{1,0:T(8,128)(2,1)} %param.18), kind=kOutput, calls=%fused_computation.18 | convolution fusion | flops 2147483648 | bytes 13107200 | tf_op jit(solution)/shard_map/dot_general | solution.py:105
  404.9 1.5 broadcast_in_dim.21
  406.4 15.5 %while.25 = (s32[]{:T(128)}, bf16[2048,512]{1,0:T(8,128)(2,1)}, s32[]{:T(128)}, s32[]{:T(128)}, bf16[2304,256]{1,0:T(8,128)(2,1)S(1)}, /*index=5*/bf16[2,256,256...) while((s32[]{:T(128)}, bf16[2048,512]{1,0:T(8,128)(2,1)}, ...), condition=%wide.region_4.0_spmd, body=%wide.region_3.0_spmd.sunk | while | flops 67633160 | bytes 3406569 | solution.py:121
  406.4 13.6 %convolution_bitcast_fusion.6 = bf16[2,1,256,256]{3,1,0,2:T(2,128)(2,1)S(1)} fusion(bf16[256,1,256,2]{2,3,0,1:T(2,128)(2,1)S(1)} %bitcast.129, bf16[1,511,256,1]{2,1,3,0:T(8,128)(2,1)S(1)} %dynamic-slice_bitcast_fusion.5), kind=kOutput, calls=%fused_computation.8.clone.1 | convolution fusion | flops 67108864 | bytes 785920 | tf_op jit(solution)/shard_map/convolution.7
  421.1 0.7 maximum_dynamic-update-slice_fusion.2
  421.9 148.9 %reduce-scatter.5.cloned.1.call-done = bf16[256,512]{1,0:T(8,128)(2,1)} async-done(((bf16[2048,512]{1,0:T(8,128)(2,1)}), bf16[256,512]{1,0:T(8,128)(2,1)}) %reduce-scatter.5.cloned.1.call-update) | async-done | bytes 262160 | tf_op jit(solution)/shard_map/reduce_scatter | solution.py:124
  570.7 1.8 fusion.40
  (47 shorter events, 4.1 us)
Async XLA Ops:
  7.2 22.2 %copy-start.1 = (bf16[256,256]{1,0:T(8,128)(2,1)S(1)}, bf16[256,256]{1,0:T(8,128)(2,1)}, u32[]{:S(2)}) copy-start(bf16[256,256]{1,0:T(8,128)(2,1)} %param.12) | copy-start | bytes 393220
  7.2 54.7 %all-gather.4.cloned.1.call-start = ((), (), s32[]{:S(2)}) async-start(), calls=%async_computation.3 | async-start | bytes 1179648 | tf_op jit(solution)/shard_map/all_gather | solution.py:52
  8.6 11.6 %collective-permute-start = (bf16[2,256]{1,0:T(2,128)(2,1)S(1)}, bf16[2,256]{1,0:T(2,128)(2,1)S(1)}, u32[]{:S(2)}, u32[]{:S(2)}) collective-permute-start(bf16[2,256]{1,0:T(2,128)(2,1)S(1)} %slice.125), channel_id=1, source_target_pairs={{0,32},{32,64},{64,96},{96,128},{128,160},{160,192},{192,224},{1,3... | collective-permute-start | bytes 3080 | tf_op jit(solution)/shard_map/ppermute | solution.py:11
  13.1 7.1 %collective-permute-start.1 = (bf16[2,256]{1,0:T(2,128)(2,1)S(1)}, bf16[2,256]{1,0:T(2,128)(2,1)S(1)}, u32[]{:S(2)}, u32[]{:S(2)}) collective-permute-start(bf16[2,256]{1,0:T(2,128)(2,1)S(1)} %slice.131), channel_id=1, source_target_pairs={{0,32},{32,64},{64,96},{96,128},{128,160},{160,192},{192,224},{1,3... | collective-permute-start | bytes 3080 | tf_op jit(solution)/shard_map/ppermute | solution.py:11
  21.5 40.3 %all-to-all-start = ((bf16[8,256,256]{2,1,0:T(8,128)(2,1)}), bf16[8,256,256]{2,1,0:T(8,128)(2,1)S(1)}, u32[]{:S(2)}, u32[]{:S(2)}) async-start(bf16[8,256,256]{2,1,0:T(8,128)(2,1)} %stack.44), calls=%async_computation | async-start | bytes 2097152 | tf_op jit(solution)/shard_map/all_to_all | solution.py:62
  28.6 72.7 %all-gather.6.cloned.1.call-start = ((), (), s32[]{:S(2)}) async-start(), calls=%async_computation.4 | async-start | bytes 1179648 | tf_op jit(solution)/shard_map/all_gather | solution.py:53
  29.3 302.2 %reduce-scatter.3.cloned.1.call-start = ((), (), s32[]{:S(2)}) async-start(), calls=%async_computation.5 | async-start | bytes 8650752 | tf_op jit(solution)/shard_map/reduce_scatter | solution.py:89
  29.4 26.8 %collective-permute-start.2 = (bf16[2,256]{1,0:T(2,128)(2,1)S(1)}, bf16[2,256]{1,0:T(2,128)(2,1)S(1)}, u32[]{:S(2)}, u32[]{:S(2)}) collective-permute-start(bf16[2,256]{1,0:T(2,128)(2,1)S(1)} %slice.137), channel_id=1, source_target_pairs={{0,32},{32,64},{64,96},{96,128},{128,160},{160,192},{192,224},{1,3... | collective-permute-start | bytes 3080 | tf_op jit(solution)/shard_map/ppermute | solution.py:11
  101.5 15.7 %copy-start = (f32[256,256]{1,0:T(8,128)S(1)}, f32[256,256]{1,0:T(8,128)}, u32[]{:S(2)}) copy-start(f32[256,256]{1,0:T(8,128)} %convert_element_type.60) | copy-start | bytes 786436
  101.5 15.7 %copy-start.2 = (f32[2,256]{1,0:T(2,128)S(1)}, f32[2,256]{1,0:T(2,128)}, u32[]{:S(2)}) copy-start(f32[2,256]{1,0:T(2,128)} %convert_element_type.61) | copy-start | bytes 6148
  101.5 15.7 %copy-start.3 = (f32[1,1,256]{2,1,0:T(1,128)S(1)}, f32[1,1,256]{2,1,0:T(1,128)}, u32[]{:S(2)}) copy-start(f32[1,1,256]{2,1,0:T(1,128)} %get-tuple-element.237) | copy-start | bytes 3076
  101.5 15.7 %copy-start.4 = (f32[1,1,256]{2,1,0:T(1,128)S(1)}, f32[1,1,256]{2,1,0:T(1,128)}, u32[]{:S(2)}) copy-start(f32[1,1,256]{2,1,0:T(1,128)} %get-tuple-element.244) | copy-start | bytes 3076
  101.5 15.7 %copy-start.5 = (f32[1,1,256]{2,1,0:T(1,128)S(1)}, f32[1,1,256]{2,1,0:T(1,128)}, u32[]{:S(2)}) copy-start(f32[1,1,256]{2,1,0:T(1,128)} %get-tuple-element.245) | copy-start | bytes 3076
  125.2 272.4 %all-gather.8.cloned.1.call-start = ((), (), s32[]{:S(2)}) async-start(), calls=%async_computation.6 | async-start | bytes 8650752 | tf_op jit(solution)/shard_map/all_gather | solution.py:107
  334.3 236.5 %reduce-scatter.5.cloned.1.call-start = ((), (), s32[]{:S(2)}) async-start(), calls=%async_computation.7 | async-start | bytes 2359296 | tf_op jit(solution)/shard_map/reduce_scatter | solution.py:124
Sparse Core Ops, SparseCore 0:
  9.8 48.7 all-gather.3
  60.3 40.9 all-gather.5
  125.3 206.1 reduce-scatter.2
  334.4 63.1 all-gather.7
  422.0 148.7 reduce-scatter.4
